TPU v7x, 256 devices: a whole 4x4x8 slice. The times are simulated.
256 devices in a mesh: row: 32 (over x, y, core), col: 8 (over z).
Axes of the slice: x: 4, y: 4, z: 8, core: 2. Of those that a mesh axis runs over, the one named last changes fastest.
Arguments:
- slab: float32 [16384, 10240], P('row', 'col'), may hold values from -6 to 6
- leaf_y: float32 [16384, 256], P('row', 'col'), may hold values from -0.25 to 0.25
- leaf_t: float32 [8192, 256], P('row', 'col'), may hold values from -0.2 to 2.3, as said below
- tree_y: float32 [5, 8192, 256], P(None, 'row'), may hold values from -0.25 to 0.25
- tree_t: float32 [5, 8192, 256], P(None, 'row'), may hold values from -0.2 to 2.3, as said below
Outputs:
- result: float32 [16384, 10240], P('row', 'col')
Inputs may be any that keep to these rules, and one draw needn't show every extreme that they name: `leaf_t`: each 256 x 256 block is upper triangular, with diagonal entries between 1.7 and 2.3 and off-diagonal entries of magnitude at most 0.2. `tree_t`: each 256 x 256 block is upper triangular, with diagonal entries between 1.7 and 2.3 and off-diagonal entries of magnitude at most 0.2; blocks of a section s that do not belong to a node's lower member are not used.
All inputs are finite; a program needn't handle non-finite values.
Results may differ from a plain program's by a relative error of at most 0.0002.
Values sent between devices are 32-bit elements; how exact they have to be, the bound alone decides.
No kernel may reach another device: no remote copies, remote signals or barrier semaphores. Data moves between devices by JAX's collectives and lax.ppermute only.
A program may use at most 64 MiB of HBM per device.

v0:
```python
import functools

import jax
import jax.numpy as jnp
from jax import lax
from jax.experimental import pallas as pl
from jax.experimental.pallas import tpu as pltpu
from jax.sharding import PartitionSpec as P


ROWS = 32
COLS = 8
LAST = 4
B = 256
HALF = 640
CHUNKS = ((0, 384), (384, 256))


F32 = jnp.float32
BF16 = jnp.bfloat16
VMEM = pl.BlockSpec(memory_space=pltpu.VMEM)
HBM = pl.BlockSpec(memory_space=pltpu.HBM)
PARAMS = pltpu.CompilerParams(vmem_limit_bytes=16 << 20)


def struct(shape, dtype=F32):
    return jax.ShapeDtypeStruct(shape, dtype)


def core_index():
    return lax.rem(lax.axis_index("row"), 2)


def is_member(section):
    row = lax.axis_index("row")
    return lax.rem(row - lax.rem(row, 2), 2**section) == 0


def is_low(section):
    return is_member(section + 1)


def near(shape, dtype=F32):
    return pltpu.VMEM(shape, dtype)


def here(*values):
    return tuple(pltpu.with_memory_space_constraint(value, pltpu.VMEM) for value in values)


def away(*values):
    return tuple(pltpu.with_memory_space_constraint(value, pltpu.HBM) for value in values)


def cost(flops, moved):
    return pl.CostEstimate(flops=flops, bytes_accessed=moved, transcendentals=0)


def split(value):
    high = value.astype(BF16)
    return high, (value - high.astype(F32)).astype(BF16)


def dot3(left, right):
    one = functools.partial(jnp.dot, preferred_element_type=F32)
    return one(left[0], right[0]) + (one(left[0], right[1]) + one(left[1], right[0]))


def leaf_top(slab, mats, out_mine, out_send, out_z, core, width):
    y_rows, y_top, tri = mats
    coeffs = dot3(y_rows, split(slab))
    scaled = split(dot3(tri, split(coeffs)))
    out_z[0] = scaled[0]
    out_z[1] = scaled[1]
    top = slab[:B] - dot3(y_top, scaled)
    left, right = top[:, :width], top[:, width:]
    out_mine[...] = jnp.where(core == 0, left, right)
    out_send[...] = jnp.where(core == 0, right, left)


def load(slab, buf, sem, start, width):
    return [
        pltpu.make_async_copy(
            slab.at[:, pl.ds(side * HALF + start, width)], buf.at[:, pl.ds(side * width, width)], sem.at[side]
        )
        for side in range(2)
    ]


def leaf_first(start, width, *refs):
    pieces = refs[:COLS]
    slab, out_mine, out_send, out_z, out_rows, out_y, out_tri, buf, full, sem = refs[COLS:]
    copies = load(slab, buf, sem, start, width)
    for copy in copies:
        copy.start()
    core, place = core_index(), lax.axis_index("col")
    count = pieces[0].shape[0]
    for step in range(COLS):
        row = pl.multiple_of(lax.rem(place + step, COLS) * count, count)
        full[pl.ds(row, count), :] = pieces[step][...]
    y_rows = full[:, : 2 * B]
    rows = split(y_rows)
    out_rows[0] = rows[0]
    out_rows[1] = rows[1]
    tri = split(full[:, 2 * B :])
    out_tri[0] = tri[0]
    out_tri[1] = tri[1]
    turned = split(y_rows.T)
    out_y[0] = turned[0]
    out_y[1] = turned[1]
    y_top = (turned[0][:B], turned[1][:B])
    for copy in copies:
        copy.wait()
    leaf_top(buf[...], (rows, y_top, tri), out_mine, out_send, out_z, core, width)


def leaf_second(start, width, slab, rows, y, tri, out_mine, out_send, out_z, buf, sem):
    copies = load(slab, buf, sem, start, width)
    for copy in copies:
        copy.start()
    for copy in copies:
        copy.wait()
    mats = ((rows[0], rows[1]), (y[0, :B], y[1, :B]), (tri[0], tri[1]))
    leaf_top(buf[...], mats, out_mine, out_send, out_z, core_index(), width)


def leaf_bottom(slab, y, *refs):
    count = len(CHUNKS)
    scaled, (out, buf, result, sem) = refs[:count], refs[count:]
    get = pltpu.make_async_copy(slab.at[pl.ds(B, B), :], buf, sem.at[0])
    get.start()
    get.wait()
    low = (y[0, B:], y[1, B:])
    for (start, size), z in zip(CHUNKS, scaled):
        change = dot3(low, (z[0], z[1]))
        for side in range(2):
            at = side * HALF + start
            result[:, at : at + size] = buf[:, at : at + size] - change[:, side * size : (side + 1) * size]
    put = pltpu.make_async_copy(result, out.at[pl.ds(B, B), :], sem.at[1])
    put.start()
    put.wait()


def keep(out, place, pair):
    out[place] = pair[0]
    out[place + 1] = pair[1]


def prepare_first(own_y, own_t, other_y, other_t, out):
    keep(out, 0, split(own_y[0].T))
    keep(out, 2, split(other_y[0].T))
    keep(out, 4, split(own_y[0]))
    keep(out, 6, split(other_y[0]))
    keep(out, 8, split(jnp.where(core_index() == 0, own_t[0], other_t[0]).T))


def prepare(section, own_y, other_y, out):
    vectors = jnp.where(core_index() == 0, own_y[0], other_y[section])
    keep(out, 0, split(vectors.T))
    keep(out, 2, split(vectors))


def prepare_factors(first, own_t, other_t, got, sent, out):
    upper = got[...] + sent[...]
    for number in range(2):
        own = jnp.where(core_index() == 0, own_t[first + number], other_t[first + number])
        keep(out, 2 * number, split(jnp.where(is_low(first + number), own, upper).T))


def section_first(mine, theirs, mats, following, out_rest, out_done, out_part):
    at = lambda place: (mats[place], mats[place + 1])
    own, other = mine[...], theirs[...]
    node = dot3(at(0), split(own)) + dot3(at(2), split(other))
    node = split(dot3(at(8), split(node)))
    own = own - dot3(at(4), node)
    other = other - dot3(at(6), node)
    rest = jnp.where(core_index() == 0, own, other)
    out_rest[...] = rest
    out_done[...] = jnp.where(core_index() == 0, other, own)
    out_part[...] = dot3((following[0], following[1]), split(rest))


def update(section, part, other, rest, mats, factor):
    at = 2 * (1 - section % 2)
    node = dot3((factor[at], factor[at + 1]), split(part[...] + other[...]))
    change = dot3((mats[2], mats[3]), split(node))
    return rest[...] - jnp.where(is_member(section), change, 0.0)


def section_next(section, part, other, rest, mats, factor, following, out_rest, out_part):
    new = update(section, part, other, rest, mats, factor)
    out_rest[...] = new
    out_part[...] = dot3((following[0], following[1]), split(new))


def section_last(section, part, other, rest, mats, factor, done, out_keep, out_send):
    new = update(section, part, other, rest, mats, factor)
    out_keep[...] = jnp.where(core_index() == 0, new, done[...])
    out_send[...] = jnp.where(core_index() == 0, done[...], new)


def finish(*refs):
    count = len(CHUNKS)
    kept, got, (_, out, sem) = refs[:count], refs[count : 2 * count], refs[2 * count :]
    for core in range(2):

        @pl.when(core_index() == core)
        def _():
            copies = []
            for number, (start, size) in enumerate(CHUNKS):
                for kind, (side, source) in enumerate(((core, kept[number]), (1 - core, got[number]))):
                    place = out.at[pl.ds(0, B), pl.ds(side * HALF + start, size)]
                    copies.append(pltpu.make_async_copy(source, place, sem.at[2 * number + kind]))
            for copy in copies:
                copy.start()
            for copy in copies:
                copy.wait()


def ring(block, step):
    return lax.ppermute(block, "col", [(i, (i + step) % COLS) for i in range(COLS)])


def pieces_of(own):
    two_below = ring(own, 2)
    two_above = ring(own, -2)
    from_below = ring(own, 1)
    from_above = ring(own, -1)
    opposite = ring(two_below, 2)
    three_below = ring(two_below, 1)
    three_above = ring(two_above, -1)
    return [own, from_above, two_above, three_above, opposite, three_below, two_below, from_below]


def pairs(section):
    stride = 2**section
    return [
        (low, low + stride)
        for base in range(0, ROWS, 2 * stride)
        for low in ((base, base + 1) if section else (base,))
    ]


def both(routes):
    return routes + [(high, low) for low, high in routes]


def call(body, outs, specs, args, scratch=(), flops=10**9, **options):
    return pl.pallas_call(
        body,
        out_shape=outs,
        in_specs=specs,
        out_specs=jax.tree.map(lambda _: HBM if options.get("far") else VMEM, outs),
        scratch_shapes=scratch,
        compiler_params=PARAMS,
        cost_estimate=cost(flops, 3 * 10**6),
        **{key: value for key, value in options.items() if key != "far"},
    )(*args)


def swap(block, routes):
    return lax.ppermute(block, "row", routes)


def shards(slab, leaf_y, leaf_t, tree_y, tree_t):
    core = core_index()
    core_pairs = both(pairs(0))

    pieces = pieces_of(jnp.concatenate([leaf_y.T, leaf_t.T], axis=1))
    other_y = swap(tree_y, core_pairs)
    other_t = swap(tree_t, core_pairs)

    def prepared(body, count, section, own, others):
        block = pl.BlockSpec((1, B, B), lambda i: (section, 0, 0))
        return pl.pallas_call(
            body,
            grid=(1,),
            out_shape=near((count, B, B), BF16),
            in_specs=[block] * len(own) + [VMEM] * len(others),
            out_specs=VMEM,
            compiler_params=PARAMS,
            cost_estimate=cost(2 * 10**8, 2 * 10**6),
        )(*away(*own), *here(*others))

    mats = [prepared(prepare_first, 10, 0, (tree_y, tree_t), (other_y, other_t))]
    for section in range(1, LAST + 1):
        body = functools.partial(prepare, section)
        mats.append(prepared(body, 4, section, (tree_y,), (other_y,)))
    factors = [None]
    for first in (1, 3):
        block = jnp.where(core == 0, tree_t[first], other_t[first + 1])
        routes = [(low, high) for low, high in pairs(first) if low % 2 == 0]
        routes += [(low, high) for low, high in pairs(first + 1) if low % 2 == 1]
        got = swap(block, routes)
        sent = swap(got, core_pairs)
        both_factors = call(
            functools.partial(prepare_factors, first),
            near((4, B, B), BF16),
            [VMEM] * 4,
            here(tree_t, other_t, got, sent),
        )
        factors += [both_factors] * 2

    rows = slab.shape[0]
    state, scaled = [], []
    for number, (start, size) in enumerate(CHUNKS):
        outs = (near((B, size)), near((B, size)), near((2, B, 2 * size), BF16))
        scratch = [pltpu.VMEM((rows, 2 * size), F32), pltpu.SemaphoreType.DMA((2,))]
        if number == 0:
            outs += (near((2, B, rows), BF16), near((2, rows, B), BF16), near((2, B, B), BF16))
            mine, send, z, y_rows, y_cols, tri = call(
                functools.partial(leaf_first, start, size),
                outs,
                [VMEM] * COLS + [HBM],
                here(*pieces) + away(slab),
                scratch[:1] + [pltpu.VMEM((B, rows + B), F32)] + scratch[1:],
            )
        else:
            mine, send, z = call(
                functools.partial(leaf_second, start, size),
                outs,
                [HBM] + [VMEM] * 3,
                away(slab) + here(y_rows, y_cols, tri),
                scratch,
            )
        scaled.append(z)
        theirs = swap(send, core_pairs)
        state.append(
            call(section_first, (near((B, size)),) * 3, [VMEM] * 4, here(mine, theirs, mats[0], mats[1]))
        )
    result = call(
        leaf_bottom,
        struct(slab.shape),
        [HBM] + [VMEM] * (1 + len(CHUNKS)),
        away(slab) + here(y_cols, *scaled),
        [pltpu.VMEM((B, 2 * HALF), F32)] * 2 + [pltpu.SemaphoreType.DMA((2,))],
        far=True,
    )
    for section in range(1, LAST + 1):
        last = section == LAST
        for number, (_, size) in enumerate(CHUNKS):
            rest, done, part = state[number]
            other = swap(part, both(pairs(section)))
            one, two = call(
                functools.partial(section_last if last else section_next, section),
                (near((B, size)),) * 2,
                [VMEM] * 6,
                here(part, other, rest, mats[section], factors[section], done if last else mats[section + 1]),
            )
            state[number] = (one, done, two)
    kept = [entry[0] for entry in state]
    got = [swap(entry[2], core_pairs) for entry in state]
    return call(
        finish,
        struct(slab.shape),
        [VMEM] * (2 * len(CHUNKS)) + [HBM],
        here(*kept, *got) + (result,),
        [pltpu.SemaphoreType.DMA((2 * len(CHUNKS),))],
        far=True,
        input_output_aliases={2 * len(CHUNKS): 0},
    )


def solution(mesh):
    in_specs = (
        P("row", "col"),
        P("row", "col"),
        P("row", "col"),
        P(None, "row", None),
        P(None, "row", None),
    )
    out_specs = P("row", "col")

    return jax.shard_map(shards, mesh=mesh, in_specs=in_specs, out_specs=out_specs, check_vma=False)
```

profile of v0, /device:TPU:1, one launch (start us, length us, event | category | flops | bytes accessed | tf_op | source)
XLA Modules:
  0.0 118.3 jit_solution(5097362388816207435)
XLA Ops:
  0.0 3.2 %collective-permute-start.9 = (f32[5,256,256]{2,1,0:T(8,128)}, f32[5,256,256]{2,1,0:T(8,128)S(1)}, u32[]{:S(2)}, u32[]{:S(2)}) collective-permute-start(f32[5,256,256]{2,1,0:T(8,128)} %own_t.5), channel_id=1, source_target_pairs={{0,8},{16,24},{32,40},{48,56},{64,72},{80,88},{96,104},{112,120},{... | collective-permute-start | bytes 3932168 | tf_op jit(solution)/shard_map/ppermute | solution.py:262
  4.1 2.9 %collective-permute-start.3 = (f32[32,768]{1,0:T(8,128)S(1)}, f32[32,768]{1,0:T(8,128)S(1)}, u32[]{:S(2)}, u32[]{:S(2)}) collective-permute-start(f32[32,768]{1,0:T(8,128)S(1)} %pad_maximum_fusion.refs_0_), channel_id=1, source_target_pairs={{0,2},{1,3},{2,4},{3,5},{4,6},{5,7},{6,0},{7,1},{8,10},{9,11},{10,... | collective-permute-start | bytes 294920 | tf_op jit(solution)/shard_map/ppermute | solution.py:221
  7.0 2.1 %collective-permute-start.1 = (f32[32,768]{1,0:T(8,128)S(1)}, f32[32,768]{1,0:T(8,128)S(1)}, u32[]{:S(2)}, u32[]{:S(2)}) collective-permute-start(f32[32,768]{1,0:T(8,128)S(1)} %pad_maximum_fusion.refs_0_), channel_id=1, source_target_pairs={{0,6},{1,7},{2,0},{3,1},{4,2},{5,3},{6,4},{7,5},{8,14},{9,15},{10,... | collective-permute-start | bytes 294920 | tf_op jit(solution)/shard_map/ppermute | solution.py:221
  11.8 2.6 %collective-permute-done.3.refs_6_ = f32[32,768]{1,0:T(8,128)S(1)} collective-permute-done((f32[32,768]{1,0:T(8,128)S(1)}, f32[32,768]{1,0:T(8,128)S(1)}, u32[]{:S(2)}, u32[]{:S(2)}) %collective-permute-start.3) | collective-permute-done | bytes 98336 | tf_op jit(solution)/shard_map/ppermute | solution.py:221
  14.7 2.3 %collective-permute-start.4 = (f32[32,768]{1,0:T(8,128)S(1)}, f32[32,768]{1,0:T(8,128)S(1)}, u32[]{:S(2)}, u32[]{:S(2)}) collective-permute-start(f32[32,768]{1,0:T(8,128)S(1)} %collective-permute-done.3.refs_6_), channel_id=1, source_target_pairs={{0,2},{1,3},{2,4},{3,5},{4,6},{5,7},{6,0},{7,1},{8,10},{9,11},{10,... | collective-permute-start | bytes 294920 | tf_op jit(solution)/shard_map/ppermute | solution.py:221
  19.1 3.1 %collective-permute-done.4.refs_4_ = f32[32,768]{1,0:T(8,128)S(1)} collective-permute-done((f32[32,768]{1,0:T(8,128)S(1)}, f32[32,768]{1,0:T(8,128)S(1)}, u32[]{:S(2)}, u32[]{:S(2)}) %collective-permute-start.4) | collective-permute-done | bytes 98336 | tf_op jit(solution)/shard_map/ppermute | solution.py:221
  22.2 4.3 %shard_map.55 = (f32[256,384]{1,0:T(8,128)S(1)}, f32[256,384]{1,0:T(8,128)}, bf16[2,256,768]{2,1,0:T(8,128)(2,1)S(1)}, bf16[2,256,512]{2,1,0:T(8,128)(2,1)S(1)},...) custom-call(f32[32,768]{1,0:T(8,128)S(1)} %pad_maximum_fusion.refs_0_, ...), custom_call_target="tpu_custom_call" | custom-call | flops 1000000000 | bytes 3000000 | tf_op jit(solution)/shard_map/pallas_call | solution.py:249
  28.9 3.4 %collective-permute-start.7 = (f32[256,384]{1,0:T(8,128)}, f32[256,384]{1,0:T(8,128)}, u32[]{:S(2)}, u32[]{:S(2)}) collective-permute-start(f32[256,384]{1,0:T(8,128)} %get-tuple-element.37), channel_id=1, source_target_pairs={{0,8},{16,24},{32,40},{48,56},{64,72},{80,88},{96,104},{112,120},{... | collective-permute-start | bytes 1179656 | tf_op jit(solution)/shard_map/ppermute | solution.py:262
  33.4 4.8 %collective-permute-start.11 = (f32[256,256]{1,0:T(8,128)S(1)}, f32[256,256]{1,0:T(8,128)S(1)}, u32[]{:S(2)}, u32[]{:S(2)}) collective-permute-start(f32[256,256]{1,0:T(8,128)S(1)} %get-tuple-element.68), channel_id=1, source_target_pairs={{0,16},{32,48},{64,80},{96,112},{128,144},{160,176},{192,208},{224... | collective-permute-start | bytes 786440 | tf_op jit(solution)/shard_map/ppermute | solution.py:262
  40.8 2.9 %shard_map.58 = (f32[256,384]{1,0:T(8,128)S(1)}, f32[256,384]{1,0:T(8,128)S(1)}, f32[256,384]{1,0:T(8,128)S(1)}) custom-call(f32[256,384]{1,0:T(8,128)S(1)} %copy-done.6, f32[256,384]{1,0:T(8,128)} %collective-permute-done.7.theirs, bf16[10,256,256]{2,1,0:T(8,128)(2,1)S(1)} %shard_map.56.mats, bf16[4,256,256]{2,1,0:T(8,128)(2,1)S(1)} %shard_map.57.following.mats), custom_call_target="tpu_custom_call" | custom-call | flops 1000000000 | bytes 3000000 | tf_op jit(solution)/shard_map/pallas_call | solution.py:249
  44.1 2.5 %shard_map.68 = (f32[256,256]{1,0:T(8,128)S(1)}, f32[256,256]{1,0:T(8,128)S(1)}, bf16[2,256,512]{2,1,0:T(8,128)(2,1)S(1)}) custom-call(f32[512,1280]{1,0:T(8,128)} %slab.3, bf16[2,256,512]{2,1,0:T(8,128)(2,1)S(1)} %copy-done.4, bf16[2,512,256]{2,1,0:T(8,128)(2,1)S(1)} %get-tuple-element.49.y, bf16[2,256,256]{2,1,0:T(8,128)(2,1)S(1)} %get-tuple-element.50.tri), custom_call_target="tpu_custom_call" | custom-call | flops 1000000000 | bytes 3000000 | tf_op jit(solution)/shard_map/pallas_call | solution.py:249
  48.6 5.2 %collective-permute-done.10.other = f32[256,384]{1,0:T(8,128)S(1)} collective-permute-done((f32[256,384]{1,0:T(8,128)S(1)}, f32[256,384]{1,0:T(8,128)S(1)}, u32[]{:S(2)}, u32[]{:S(2)}) %collective-permute-start.10) | collective-permute-done | bytes 393248 | tf_op jit(solution)/shard_map/ppermute | solution.py:262
  58.4 4.7 %collective-permute-start.15 = (f32[256,256]{1,0:T(8,128)S(1)}, f32[256,256]{1,0:T(8,128)S(1)}, u32[]{:S(2)}, u32[]{:S(2)}) collective-permute-start(f32[256,256]{1,0:T(8,128)S(1)} %get-tuple-element.67), channel_id=1, source_target_pairs={{0,64},{128,192},{8,136},{1,65},{129,193},{9,137},{2,66},{130,194}... | collective-permute-start | bytes 786440 | tf_op jit(solution)/shard_map/ppermute | solution.py:262
  64.2 5.7 %collective-permute-done.19.other = f32[256,256]{1,0:T(8,128)S(1)} collective-permute-done((f32[256,256]{1,0:T(8,128)S(1)}, f32[256,256]{1,0:T(8,128)S(1)}, u32[]{:S(2)}, u32[]{:S(2)}) %collective-permute-start.19) | collective-permute-done | bytes 262176 | tf_op jit(solution)/shard_map/ppermute | solution.py:262
  70.8 6.0 %collective-permute-start.20 = (f32[256,256]{1,0:T(8,128)S(1)}, f32[256,256]{1,0:T(8,128)S(1)}, u32[]{:S(2)}, u32[]{:S(2)}) collective-permute-start(f32[256,256]{1,0:T(8,128)S(1)} %get-tuple-element.55.part), channel_id=1, source_target_pairs={{0,32},{8,40},{64,96},{72,104},{128,160},{136,168},{192,224},{200,... | collective-permute-start | bytes 786440 | tf_op jit(solution)/shard_map/ppermute | solution.py:262
  77.8 3.1 %collective-permute-start.14 = (f32[256,384]{1,0:T(8,128)S(1)}, f32[256,384]{1,0:T(8,128)S(1)}, u32[]{:S(2)}, u32[]{:S(2)}) collective-permute-start(f32[256,384]{1,0:T(8,128)S(1)} %get-tuple-element.42.part), channel_id=1, source_target_pairs={{0,64},{8,72},{128,192},{136,200},{64,0},{72,8},{192,128},{200,136... | collective-permute-start | bytes 1179656 | tf_op jit(solution)/shard_map/ppermute | solution.py:262
  84.3 2.2 %collective-permute-start.21 = (f32[256,256]{1,0:T(8,128)S(1)}, f32[256,256]{1,0:T(8,128)S(1)}, u32[]{:S(2)}, u32[]{:S(2)}) collective-permute-start(f32[256,256]{1,0:T(8,128)S(1)} %get-tuple-element.57.part), channel_id=1, source_target_pairs={{0,64},{8,72},{128,192},{136,200},{64,0},{72,8},{192,128},{200,136... | collective-permute-start | bytes 786440 | tf_op jit(solution)/shard_map/ppermute | solution.py:262
  86.8 2.7 %collective-permute-done.14.other = f32[256,384]{1,0:T(8,128)S(1)} collective-permute-done((f32[256,384]{1,0:T(8,128)S(1)}, f32[256,384]{1,0:T(8,128)S(1)}, u32[]{:S(2)}, u32[]{:S(2)}) %collective-permute-start.14) | collective-permute-done | bytes 393248 | tf_op jit(solution)/shard_map/ppermute | solution.py:262
  90.5 4.7 %collective-permute-start.17 = (f32[256,384]{1,0:T(8,128)S(1)}, f32[256,384]{1,0:T(8,128)S(1)}, u32[]{:S(2)}, u32[]{:S(2)}) collective-permute-start(f32[256,384]{1,0:T(8,128)S(1)} %get-tuple-element.44.part), channel_id=1, source_target_pairs={{0,128},{8,136},{128,0},{136,8},{1,129},{9,137},{129,1},{137,9},{2... | collective-permute-start | bytes 1179656 | tf_op jit(solution)/shard_map/ppermute | solution.py:262
  96.1 4.6 %collective-permute-start.22 = (f32[256,256]{1,0:T(8,128)S(1)}, f32[256,256]{1,0:T(8,128)S(1)}, u32[]{:S(2)}, u32[]{:S(2)}) collective-permute-start(f32[256,256]{1,0:T(8,128)S(1)} %get-tuple-element.59.part), channel_id=1, source_target_pairs={{0,128},{8,136},{128,0},{136,8},{1,129},{9,137},{129,1},{137,9},{2... | collective-permute-start | bytes 786440 | tf_op jit(solution)/shard_map/ppermute | solution.py:262
  100.7 4.8 %collective-permute-done.17.other = f32[256,384]{1,0:T(8,128)S(1)} collective-permute-done((f32[256,384]{1,0:T(8,128)S(1)}, f32[256,384]{1,0:T(8,128)S(1)}, u32[]{:S(2)}, u32[]{:S(2)}) %collective-permute-start.17) | collective-permute-done | bytes 393248 | tf_op jit(solution)/shard_map/ppermute | solution.py:262
  106.2 3.7 %collective-permute-start.23 = (f32[256,384]{1,0:T(8,128)S(1)}, f32[256,384]{1,0:T(8,128)S(1)}, u32[]{:S(2)}, u32[]{:S(2)}) collective-permute-start(f32[256,384]{1,0:T(8,128)S(1)} %get-tuple-element.63), channel_id=1, source_target_pairs={{0,8},{16,24},{32,40},{48,56},{64,72},{80,88},{96,104},{112,120},{... | collective-permute-start | bytes 1179656 | tf_op jit(solution)/shard_map/ppermute | solution.py:262
  111.8 2.1 %collective-permute-start.24 = (f32[256,256]{1,0:T(8,128)S(1)}, f32[256,256]{1,0:T(8,128)S(1)}, u32[]{:S(2)}, u32[]{:S(2)}) collective-permute-start(f32[256,256]{1,0:T(8,128)S(1)} %get-tuple-element.64), channel_id=1, source_target_pairs={{0,8},{16,24},{32,40},{48,56},{64,72},{80,88},{96,104},{112,120},{... | collective-permute-start | bytes 786440 | tf_op jit(solution)/shard_map/ppermute | solution.py:262
  113.9 3.1 %shard_map.74.refs_4_ = f32[512,1280]{1,0:T(8,128)} custom-call(f32[512,1280]{1,0:T(8,128)} %slab.3, bf16[2,512,256]{2,1,0:T(8,128)(2,1)S(1)} %get-tuple-element.49.y, bf16[2,256,768]{2,1,0:T(8,128)(2,1)S(1)} %copy-done.2, bf16[2,256,512]{2,1,0:T(8,128)(2,1)S(1)} %get-tuple-element.66.refs_1_), custom_call_target="tpu_custom_call" | custom-call | flops 1000000000 | bytes 3000000 | tf_op jit(solution)/shard_map/pallas_call | solution.py:249
  (63 shorter events, 31.0 us)
Async XLA Ops:
  0.0 32.3 %collective-permute-start.9 = (f32[5,256,256]{2,1,0:T(8,128)}, f32[5,256,256]{2,1,0:T(8,128)S(1)}, u32[]{:S(2)}, u32[]{:S(2)}) collective-permute-start(f32[5,256,256]{2,1,0:T(8,128)} %own_t.5), channel_id=1, source_target_pairs={{0,8},{16,24},{32,40},{48,56},{64,72},{80,88},{96,104},{112,120},{... | collective-permute-start | bytes 3932168 | tf_op jit(solution)/shard_map/ppermute | solution.py:262
  3.2 35.1 %collective-permute-start.8 = (f32[5,256,256]{2,1,0:T(8,128)}, f32[5,256,256]{2,1,0:T(8,128)S(1)}, u32[]{:S(2)}, u32[]{:S(2)}) collective-permute-start(f32[5,256,256]{2,1,0:T(8,128)} %own_y.9), channel_id=1, source_target_pairs={{0,8},{16,24},{32,40},{48,56},{64,72},{80,88},{96,104},{112,120},{... | collective-permute-start | bytes 3932168 | tf_op jit(solution)/shard_map/ppermute | solution.py:262
  4.1 6.6 %collective-permute-start.6 = (f32[32,768]{1,0:T(8,128)S(1)}, f32[32,768]{1,0:T(8,128)S(1)}, u32[]{:S(2)}, u32[]{:S(2)}) collective-permute-start(f32[32,768]{1,0:T(8,128)S(1)} %pad_maximum_fusion.refs_0_), channel_id=1, source_target_pairs={{0,1},{1,2},{2,3},{3,4},{4,5},{5,6},{6,7},{7,0},{8,9},{9,10},{10,1... | collective-permute-start | bytes 294920 | tf_op jit(solution)/shard_map/ppermute | solution.py:221
  4.1 10.3 %collective-permute-start.3 = (f32[32,768]{1,0:T(8,128)S(1)}, f32[32,768]{1,0:T(8,128)S(1)}, u32[]{:S(2)}, u32[]{:S(2)}) collective-permute-start(f32[32,768]{1,0:T(8,128)S(1)} %pad_maximum_fusion.refs_0_), channel_id=1, source_target_pairs={{0,2},{1,3},{2,4},{3,5},{4,6},{5,7},{6,0},{7,1},{8,10},{9,11},{10,... | collective-permute-start | bytes 294920 | tf_op jit(solution)/shard_map/ppermute | solution.py:221
  7.0 7.6 %collective-permute-start.1 = (f32[32,768]{1,0:T(8,128)S(1)}, f32[32,768]{1,0:T(8,128)S(1)}, u32[]{:S(2)}, u32[]{:S(2)}) collective-permute-start(f32[32,768]{1,0:T(8,128)S(1)} %pad_maximum_fusion.refs_0_), channel_id=1, source_target_pairs={{0,6},{1,7},{2,0},{3,1},{4,2},{5,3},{6,4},{7,5},{8,14},{9,15},{10,... | collective-permute-start | bytes 294920 | tf_op jit(solution)/shard_map/ppermute | solution.py:221
  10.7 6.4 %collective-permute-start = (f32[32,768]{1,0:T(8,128)S(1)}, f32[32,768]{1,0:T(8,128)S(1)}, u32[]{:S(2)}, u32[]{:S(2)}) collective-permute-start(f32[32,768]{1,0:T(8,128)S(1)} %pad_maximum_fusion.refs_0_), channel_id=1, source_target_pairs={{0,7},{1,0},{2,1},{3,2},{4,3},{5,4},{6,5},{7,6},{8,15},{9,8},{10,9... | collective-permute-start | bytes 294920 | tf_op jit(solution)/shard_map/ppermute | solution.py:221
  14.4 4.7 %collective-permute-start.5 = (f32[32,768]{1,0:T(8,128)S(1)}, f32[32,768]{1,0:T(8,128)S(1)}, u32[]{:S(2)}, u32[]{:S(2)}) collective-permute-start(f32[32,768]{1,0:T(8,128)S(1)} %collective-permute-done.3.refs_6_), channel_id=1, source_target_pairs={{0,1},{1,2},{2,3},{3,4},{4,5},{5,6},{6,7},{7,0},{8,9},{9,10},{10,1... | collective-permute-start | bytes 294920 | tf_op jit(solution)/shard_map/ppermute | solution.py:221
  14.7 7.5 %collective-permute-start.4 = (f32[32,768]{1,0:T(8,128)S(1)}, f32[32,768]{1,0:T(8,128)S(1)}, u32[]{:S(2)}, u32[]{:S(2)}) collective-permute-start(f32[32,768]{1,0:T(8,128)S(1)} %collective-permute-done.3.refs_6_), channel_id=1, source_target_pairs={{0,2},{1,3},{2,4},{3,5},{4,6},{5,7},{6,0},{7,1},{8,10},{9,11},{10,... | collective-permute-start | bytes 294920 | tf_op jit(solution)/shard_map/ppermute | solution.py:221
  17.0 5.2 %collective-permute-start.2 = (f32[32,768]{1,0:T(8,128)S(1)}, f32[32,768]{1,0:T(8,128)S(1)}, u32[]{:S(2)}, u32[]{:S(2)}) collective-permute-start(f32[32,768]{1,0:T(8,128)S(1)} %collective-permute-done.1.refs_2_), channel_id=1, source_target_pairs={{0,7},{1,0},{2,1},{3,2},{4,3},{5,4},{6,5},{7,6},{8,15},{9,8},{10,9... | collective-permute-start | bytes 294920 | tf_op jit(solution)/shard_map/ppermute | solution.py:221
  28.9 11.9 %collective-permute-start.7 = (f32[256,384]{1,0:T(8,128)}, f32[256,384]{1,0:T(8,128)}, u32[]{:S(2)}, u32[]{:S(2)}) collective-permute-start(f32[256,384]{1,0:T(8,128)} %get-tuple-element.37), channel_id=1, source_target_pairs={{0,8},{16,24},{32,40},{48,56},{64,72},{80,88},{96,104},{112,120},{... | collective-permute-start | bytes 1179656 | tf_op jit(solution)/shard_map/ppermute | solution.py:262
  33.4 10.4 %collective-permute-start.11 = (f32[256,256]{1,0:T(8,128)S(1)}, f32[256,256]{1,0:T(8,128)S(1)}, u32[]{:S(2)}, u32[]{:S(2)}) collective-permute-start(f32[256,256]{1,0:T(8,128)S(1)} %get-tuple-element.68), channel_id=1, source_target_pairs={{0,16},{32,48},{64,80},{96,112},{128,144},{160,176},{192,208},{224... | collective-permute-start | bytes 786440 | tf_op jit(solution)/shard_map/ppermute | solution.py:262
  43.7 10.1 %collective-permute-start.10 = (f32[256,384]{1,0:T(8,128)S(1)}, f32[256,384]{1,0:T(8,128)S(1)}, u32[]{:S(2)}, u32[]{:S(2)}) collective-permute-start(f32[256,384]{1,0:T(8,128)S(1)} %get-tuple-element.38.part), channel_id=1, source_target_pairs={{0,16},{8,24},{32,48},{40,56},{64,80},{72,88},{96,112},{104,120},{... | collective-permute-start | bytes 1179656 | tf_op jit(solution)/shard_map/ppermute | solution.py:262
  46.6 10.1 %collective-permute-start.18 = (f32[256,256]{1,0:T(8,128)S(1)}, f32[256,256]{1,0:T(8,128)S(1)}, u32[]{:S(2)}, u32[]{:S(2)}) collective-permute-start(f32[256,256]{1,0:T(8,128)S(1)} %get-tuple-element.52), channel_id=1, source_target_pairs={{0,8},{16,24},{32,40},{48,56},{64,72},{80,88},{96,104},{112,120},{... | collective-permute-start | bytes 786440 | tf_op jit(solution)/shard_map/ppermute | solution.py:262
  54.8 22.0 %collective-permute-start.13 = (f32[256,384]{1,0:T(8,128)S(1)}, f32[256,384]{1,0:T(8,128)S(1)}, u32[]{:S(2)}, u32[]{:S(2)}) collective-permute-start(f32[256,384]{1,0:T(8,128)S(1)} %get-tuple-element.40.part), channel_id=1, source_target_pairs={{0,32},{8,40},{64,96},{72,104},{128,160},{136,168},{192,224},{200,... | collective-permute-start | bytes 1179656 | tf_op jit(solution)/shard_map/ppermute | solution.py:262
  58.3 11.6 %collective-permute-start.19 = (f32[256,256]{1,0:T(8,128)S(1)}, f32[256,256]{1,0:T(8,128)S(1)}, u32[]{:S(2)}, u32[]{:S(2)}) collective-permute-start(f32[256,256]{1,0:T(8,128)S(1)} %get-tuple-element.53.part), channel_id=1, source_target_pairs={{0,16},{8,24},{32,48},{40,56},{64,80},{72,88},{96,112},{104,120},{... | collective-permute-start | bytes 786440 | tf_op jit(solution)/shard_map/ppermute | solution.py:262
  58.4 22.6 %collective-permute-start.15 = (f32[256,256]{1,0:T(8,128)S(1)}, f32[256,256]{1,0:T(8,128)S(1)}, u32[]{:S(2)}, u32[]{:S(2)}) collective-permute-start(f32[256,256]{1,0:T(8,128)S(1)} %get-tuple-element.67), channel_id=1, source_target_pairs={{0,64},{128,192},{8,136},{1,65},{129,193},{9,137},{2,66},{130,194}... | collective-permute-start | bytes 786440 | tf_op jit(solution)/shard_map/ppermute | solution.py:262
  70.8 12.6 %collective-permute-start.20 = (f32[256,256]{1,0:T(8,128)S(1)}, f32[256,256]{1,0:T(8,128)S(1)}, u32[]{:S(2)}, u32[]{:S(2)}) collective-permute-start(f32[256,256]{1,0:T(8,128)S(1)} %get-tuple-element.55.part), channel_id=1, source_target_pairs={{0,32},{8,40},{64,96},{72,104},{128,160},{136,168},{192,224},{200,... | collective-permute-start | bytes 786440 | tf_op jit(solution)/shard_map/ppermute | solution.py:262
  77.8 11.6 %collective-permute-start.14 = (f32[256,384]{1,0:T(8,128)S(1)}, f32[256,384]{1,0:T(8,128)S(1)}, u32[]{:S(2)}, u32[]{:S(2)}) collective-permute-start(f32[256,384]{1,0:T(8,128)S(1)} %get-tuple-element.42.part), channel_id=1, source_target_pairs={{0,64},{8,72},{128,192},{136,200},{64,0},{72,8},{192,128},{200,136... | collective-permute-start | bytes 1179656 | tf_op jit(solution)/shard_map/ppermute | solution.py:262
  81.0 5.6 %collective-permute-start.16 = (f32[256,256]{1,0:T(8,128)S(1)}, f32[256,256]{1,0:T(8,128)S(1)}, u32[]{:S(2)}, u32[]{:S(2)}) collective-permute-start(f32[256,256]{1,0:T(8,128)S(1)} %collective-permute-done.15.got), channel_id=1, source_target_pairs={{0,8},{16,24},{32,40},{48,56},{64,72},{80,88},{96,104},{112,120},{... | collective-permute-start | bytes 786440 | tf_op jit(solution)/shard_map/ppermute | solution.py:262
  84.3 10.9 %collective-permute-start.21 = (f32[256,256]{1,0:T(8,128)S(1)}, f32[256,256]{1,0:T(8,128)S(1)}, u32[]{:S(2)}, u32[]{:S(2)}) collective-permute-start(f32[256,256]{1,0:T(8,128)S(1)} %get-tuple-element.57.part), channel_id=1, source_target_pairs={{0,64},{8,72},{128,192},{136,200},{64,0},{72,8},{192,128},{200,136... | collective-permute-start | bytes 786440 | tf_op jit(solution)/shard_map/ppermute | solution.py:262
  90.5 15.0 %collective-permute-start.17 = (f32[256,384]{1,0:T(8,128)S(1)}, f32[256,384]{1,0:T(8,128)S(1)}, u32[]{:S(2)}, u32[]{:S(2)}) collective-permute-start(f32[256,384]{1,0:T(8,128)S(1)} %get-tuple-element.44.part), channel_id=1, source_target_pairs={{0,128},{8,136},{128,0},{136,8},{1,129},{9,137},{129,1},{137,9},{2... | collective-permute-start | bytes 1179656 | tf_op jit(solution)/shard_map/ppermute | solution.py:262
  96.1 15.0 %collective-permute-start.22 = (f32[256,256]{1,0:T(8,128)S(1)}, f32[256,256]{1,0:T(8,128)S(1)}, u32[]{:S(2)}, u32[]{:S(2)}) collective-permute-start(f32[256,256]{1,0:T(8,128)S(1)} %get-tuple-element.59.part), channel_id=1, source_target_pairs={{0,128},{8,136},{128,0},{136,8},{1,129},{9,137},{129,1},{137,9},{2... | collective-permute-start | bytes 786440 | tf_op jit(solution)/shard_map/ppermute | solution.py:262
  106.2 10.8 %collective-permute-start.23 = (f32[256,384]{1,0:T(8,128)S(1)}, f32[256,384]{1,0:T(8,128)S(1)}, u32[]{:S(2)}, u32[]{:S(2)}) collective-permute-start(f32[256,384]{1,0:T(8,128)S(1)} %get-tuple-element.63), channel_id=1, source_target_pairs={{0,8},{16,24},{32,40},{48,56},{64,72},{80,88},{96,104},{112,120},{... | collective-permute-start | bytes 1179656 | tf_op jit(solution)/shard_map/ppermute | solution.py:262
  111.8 5.2 %collective-permute-start.24 = (f32[256,256]{1,0:T(8,128)S(1)}, f32[256,256]{1,0:T(8,128)S(1)}, u32[]{:S(2)}, u32[]{:S(2)}) collective-permute-start(f32[256,256]{1,0:T(8,128)S(1)} %get-tuple-element.64), channel_id=1, source_target_pairs={{0,8},{16,24},{32,40},{48,56},{64,72},{80,88},{96,104},{112,120},{... | collective-permute-start | bytes 786440 | tf_op jit(solution)/shard_map/ppermute | solution.py:262
  (8 other events, 15.8 us)
where the time goes:
time: 119 us; the launch traced here: 118 us
  starting transfers between devices  56.6 us (48%)
  Pallas kernels  28.9 us (24%)
  waiting for transfers between devices  27.8 us (23%)
  local copies, waits for them, and re-layouts  2.44 us (2%)
  other arithmetic  1.97 us (2%)
    ppermute x18, starting transfers between devices, swap(): return lax.ppermute(block, 'row', routes)  46.7 us
    pallas_call x16, Pallas kernels, call(): pl.pallas_call(body, out_shape=outs, in_specs=specs, out_specs=jax.tree.m...  23.1 us
    ppermute x18, waiting for transfers between devices, swap(): return lax.ppermute(block, 'row', routes)  19.7 us
    ppermute x7, starting transfers between devices, ring(): lax.ppermute(block, 'col', [(i, (i + step) % COLS) for i in range(COLS)])  9.92 us
    ppermute x7, waiting for transfers between devices, ring(): lax.ppermute(block, 'col', [(i, (i + step) % COLS) for i in range(COLS)])  8.16 us
    pallas_call x5, Pallas kernels, prepared(): pl.pallas_call(body, grid=(1,), out_shape=near((count, B, B), BF16), in_s...  5.8 us
    unnamed x14, local copies, waits for them, and re-layouts  2.44 us
  transfers between devices with their start and end apart: 25, of which 9 were waited for; matrix products, arithmetic and copies ran while one was open for 2% of the time, Pallas kernels for 23%

commit v1 on v0

--- a/solution.py
+++ b/solution.py
@@ -199,18 +199,16 @@
     out_send[...] = jnp.where(core_index() == 0, done[...], new)
 
 
-def finish(*refs):
-    count = len(CHUNKS)
-    kept, got, (_, out, sem) = refs[:count], refs[count : 2 * count], refs[2 * count :]
+def finish(number, kept, got, _, out, sem):
+    start, size = CHUNKS[number]
     for core in range(2):
 
         @pl.when(core_index() == core)
         def _():
             copies = []
-            for number, (start, size) in enumerate(CHUNKS):
-                for kind, (side, source) in enumerate(((core, kept[number]), (1 - core, got[number]))):
-                    place = out.at[pl.ds(0, B), pl.ds(side * HALF + start, size)]
-                    copies.append(pltpu.make_async_copy(source, place, sem.at[2 * number + kind]))
+            for kind, (side, source) in enumerate(((core, kept), (1 - core, got))):
+                place = out.at[pl.ds(0, B), pl.ds(side * HALF + start, size)]
+                copies.append(pltpu.make_async_copy(source, place, sem.at[kind]))
             for copy in copies:
                 copy.start()
             for copy in copies:
@@ -348,17 +346,18 @@
                 here(part, other, rest, mats[section], factors[section], done if last else mats[section + 1]),
             )
             state[number] = (one, done, two)
-    kept = [entry[0] for entry in state]
     got = [swap(entry[2], core_pairs) for entry in state]
-    return call(
-        finish,
-        struct(slab.shape),
-        [VMEM] * (2 * len(CHUNKS)) + [HBM],
-        here(*kept, *got) + (result,),
-        [pltpu.SemaphoreType.DMA((2 * len(CHUNKS),))],
-        far=True,
-        input_output_aliases={2 * len(CHUNKS): 0},
-    )
+    for number, entry in enumerate(state):
+        result = call(
+            functools.partial(finish, number),
+            struct(slab.shape),
+            [VMEM] * 2 + [HBM],
+            here(entry[0], got[number]) + (result,),
+            [pltpu.SemaphoreType.DMA((2,))],
+            far=True,
+            input_output_aliases={2: 0},
+        )
+    return result
 
 
 def solution(mesh):

time: 119 us -> 118 us (level)
  starting transfers between devices: 56.6 us -> 54 us
    ppermute x18, starting transfers between devices: 46.7 us -> 44.1 us  [swap(): return lax.ppermute(block, 'row', routes)]
    pallas_call x16 -> x17, Pallas kernels: 23.1 us -> 23.7 us  [call(): pl.pallas_call(body, out_shape=outs, in_specs=specs, out_specs=jax.tree.m...]
  transfers between devices with their start and end apart: 25 -> 25, of which waited for: 9 -> 9; matrix products, arithmetic and copies ran while one was open for 2% -> 2% of each run, Pallas kernels for 23% -> 24%
where the time goes in v1:
time: 118 us; the launch traced here: 117 us
  starting transfers between devices  54 us (46%)
  Pallas kernels  29.5 us (25%)
  waiting for transfers between devices  28.7 us (24%)
  local copies, waits for them, and re-layouts  2.44 us (2%)
  other arithmetic  1.97 us (2%)
    ppermute x18, starting transfers between devices, swap(): return lax.ppermute(block, 'row', routes)  44.1 us
    pallas_call x17, Pallas kernels, call(): pl.pallas_call(body, out_shape=outs, in_specs=specs, out_specs=jax.tree.m...  23.7 us
    ppermute x18, waiting for transfers between devices, swap(): return lax.ppermute(block, 'row', routes)  20.5 us
    ppermute x7, starting transfers between devices, ring(): lax.ppermute(block, 'col', [(i, (i + step) % COLS) for i in range(COLS)])  9.92 us
    ppermute x7, waiting for transfers between devices, ring(): lax.ppermute(block, 'col', [(i, (i + step) % COLS) for i in range(COLS)])  8.16 us
    pallas_call x5, Pallas kernels, prepared(): pl.pallas_call(body, grid=(1,), out_shape=near((count, B, B), BF16), in_s...  5.8 us
    unnamed x14, local copies, waits for them, and re-layouts  2.44 us
  transfers between devices with their start and end apart: 25, of which 9 were waited for; matrix products, arithmetic and copies ran while one was open for 2% of the time, Pallas kernels for 24%

profile of v1, /device:TPU:1, one launch (start us, length us, event | category | flops | bytes accessed | tf_op | source)
XLA Modules:
  0.0 117.1 jit_solution(8872299833285436023)
XLA Ops:
  0.0 3.2 %collective-permute-start.9 = (f32[5,256,256]{2,1,0:T(8,128)}, f32[5,256,256]{2,1,0:T(8,128)S(1)}, u32[]{:S(2)}, u32[]{:S(2)}) collective-permute-start(f32[5,256,256]{2,1,0:T(8,128)} %own_t.5), channel_id=1, source_target_pairs={{0,8},{16,24},{32,40},{48,56},{64,72},{80,88},{96,104},{112,120},{... | collective-permute-start | bytes 3932168 | tf_op jit(solution)/shard_map/ppermute | solution.py:260
  4.1 2.9 %collective-permute-start.3 = (f32[32,768]{1,0:T(8,128)S(1)}, f32[32,768]{1,0:T(8,128)S(1)}, u32[]{:S(2)}, u32[]{:S(2)}) collective-permute-start(f32[32,768]{1,0:T(8,128)S(1)} %pad_maximum_fusion.refs_0_), channel_id=1, source_target_pairs={{0,2},{1,3},{2,4},{3,5},{4,6},{5,7},{6,0},{7,1},{8,10},{9,11},{10,... | collective-permute-start | bytes 294920 | tf_op jit(solution)/shard_map/ppermute | solution.py:219
  7.0 2.1 %collective-permute-start.1 = (f32[32,768]{1,0:T(8,128)S(1)}, f32[32,768]{1,0:T(8,128)S(1)}, u32[]{:S(2)}, u32[]{:S(2)}) collective-permute-start(f32[32,768]{1,0:T(8,128)S(1)} %pad_maximum_fusion.refs_0_), channel_id=1, source_target_pairs={{0,6},{1,7},{2,0},{3,1},{4,2},{5,3},{6,4},{7,5},{8,14},{9,15},{10,... | collective-permute-start | bytes 294920 | tf_op jit(solution)/shard_map/ppermute | solution.py:219
  11.8 2.6 %collective-permute-done.3.refs_6_ = f32[32,768]{1,0:T(8,128)S(1)} collective-permute-done((f32[32,768]{1,0:T(8,128)S(1)}, f32[32,768]{1,0:T(8,128)S(1)}, u32[]{:S(2)}, u32[]{:S(2)}) %collective-permute-start.3) | collective-permute-done | bytes 98336 | tf_op jit(solution)/shard_map/ppermute | solution.py:219
  14.7 2.3 %collective-permute-start.4 = (f32[32,768]{1,0:T(8,128)S(1)}, f32[32,768]{1,0:T(8,128)S(1)}, u32[]{:S(2)}, u32[]{:S(2)}) collective-permute-start(f32[32,768]{1,0:T(8,128)S(1)} %collective-permute-done.3.refs_6_), channel_id=1, source_target_pairs={{0,2},{1,3},{2,4},{3,5},{4,6},{5,7},{6,0},{7,1},{8,10},{9,11},{10,... | collective-permute-start | bytes 294920 | tf_op jit(solution)/shard_map/ppermute | solution.py:219
  19.1 3.1 %collective-permute-done.4.refs_4_ = f32[32,768]{1,0:T(8,128)S(1)} collective-permute-done((f32[32,768]{1,0:T(8,128)S(1)}, f32[32,768]{1,0:T(8,128)S(1)}, u32[]{:S(2)}, u32[]{:S(2)}) %collective-permute-start.4) | collective-permute-done | bytes 98336 | tf_op jit(solution)/shard_map/ppermute | solution.py:219
  22.2 4.3 %shard_map.55 = (f32[256,384]{1,0:T(8,128)S(1)}, f32[256,384]{1,0:T(8,128)}, bf16[2,256,768]{2,1,0:T(8,128)(2,1)S(1)}, bf16[2,256,512]{2,1,0:T(8,128)(2,1)S(1)},...) custom-call(f32[32,768]{1,0:T(8,128)S(1)} %pad_maximum_fusion.refs_0_, ...), custom_call_target="tpu_custom_call" | custom-call | flops 1000000000 | bytes 3000000 | tf_op jit(solution)/shard_map/pallas_call | solution.py:247
  28.9 3.4 %collective-permute-start.19 = (f32[256,384]{1,0:T(8,128)}, f32[256,384]{1,0:T(8,128)}, u32[]{:S(2)}, u32[]{:S(2)}) collective-permute-start(f32[256,384]{1,0:T(8,128)} %get-tuple-element.53), channel_id=1, source_target_pairs={{0,8},{16,24},{32,40},{48,56},{64,72},{80,88},{96,104},{112,120},{... | collective-permute-start | bytes 1179656 | tf_op jit(solution)/shard_map/ppermute | solution.py:260
  33.4 4.8 %collective-permute-start.11 = (f32[256,256]{1,0:T(8,128)S(1)}, f32[256,256]{1,0:T(8,128)S(1)}, u32[]{:S(2)}, u32[]{:S(2)}) collective-permute-start(f32[256,256]{1,0:T(8,128)S(1)} %get-tuple-element.68), channel_id=1, source_target_pairs={{0,16},{32,48},{64,80},{96,112},{128,144},{160,176},{192,208},{224... | collective-permute-start | bytes 786440 | tf_op jit(solution)/shard_map/ppermute | solution.py:260
  40.8 2.9 %shard_map.69 = (f32[256,384]{1,0:T(8,128)S(1)}, f32[256,384]{1,0:T(8,128)S(1)}, f32[256,384]{1,0:T(8,128)S(1)}) custom-call(f32[256,384]{1,0:T(8,128)S(1)} %copy-done.6, f32[256,384]{1,0:T(8,128)} %collective-permute-done.19.theirs, bf16[10,256,256]{2,1,0:T(8,128)(2,1)S(1)} %shard_map.57.mats, bf16[4,256,256]{2,1,0:T(8,128)(2,1)S(1)} %shard_map.58.following.mats), custom_call_target="tpu_custom_call" | custom-call | flops 1000000000 | bytes 3000000 | tf_op jit(solution)/shard_map/pallas_call | solution.py:247
  44.1 2.5 %shard_map.56 = (f32[256,256]{1,0:T(8,128)S(1)}, f32[256,256]{1,0:T(8,128)S(1)}, bf16[2,256,512]{2,1,0:T(8,128)(2,1)S(1)}) custom-call(f32[512,1280]{1,0:T(8,128)} %slab.3, bf16[2,256,512]{2,1,0:T(8,128)(2,1)S(1)} %copy-done.4, bf16[2,512,256]{2,1,0:T(8,128)(2,1)S(1)} %get-tuple-element.37.y, bf16[2,256,256]{2,1,0:T(8,128)(2,1)S(1)} %get-tuple-element.38.tri), custom_call_target="tpu_custom_call" | custom-call | flops 1000000000 | bytes 3000000 | tf_op jit(solution)/shard_map/pallas_call | solution.py:247
  48.6 5.2 %collective-permute-done.20.other = f32[256,384]{1,0:T(8,128)S(1)} collective-permute-done((f32[256,384]{1,0:T(8,128)S(1)}, f32[256,384]{1,0:T(8,128)S(1)}, u32[]{:S(2)}, u32[]{:S(2)}) %collective-permute-start.20) | collective-permute-done | bytes 393248 | tf_op jit(solution)/shard_map/ppermute | solution.py:260
  56.7 4.7 %collective-permute-start.15 = (f32[256,256]{1,0:T(8,128)S(1)}, f32[256,256]{1,0:T(8,128)S(1)}, u32[]{:S(2)}, u32[]{:S(2)}) collective-permute-start(f32[256,256]{1,0:T(8,128)S(1)} %get-tuple-element.67), channel_id=1, source_target_pairs={{0,64},{128,192},{8,136},{1,65},{129,193},{9,137},{2,66},{130,194}... | collective-permute-start | bytes 786440 | tf_op jit(solution)/shard_map/ppermute | solution.py:260
  64.2 3.2 %collective-permute-done.15.got = f32[256,256]{1,0:T(8,128)S(1)} collective-permute-done((f32[256,256]{1,0:T(8,128)S(1)}, f32[256,256]{1,0:T(8,128)S(1)}, u32[]{:S(2)}, u32[]{:S(2)}) %collective-permute-start.15) | collective-permute-done | bytes 262176 | tf_op jit(solution)/shard_map/ppermute | solution.py:260
  70.1 3.1 %collective-permute-start.22 = (f32[256,384]{1,0:T(8,128)S(1)}, f32[256,384]{1,0:T(8,128)S(1)}, u32[]{:S(2)}, u32[]{:S(2)}) collective-permute-start(f32[256,384]{1,0:T(8,128)S(1)} %get-tuple-element.58.part), channel_id=1, source_target_pairs={{0,64},{8,72},{128,192},{136,200},{64,0},{72,8},{192,128},{200,136... | collective-permute-start | bytes 1179656 | tf_op jit(solution)/shard_map/ppermute | solution.py:260
  74.2 2.6 %collective-permute-start.13 = (f32[256,256]{1,0:T(8,128)S(1)}, f32[256,256]{1,0:T(8,128)S(1)}, u32[]{:S(2)}, u32[]{:S(2)}) collective-permute-start(f32[256,256]{1,0:T(8,128)S(1)} %get-tuple-element.43.part), channel_id=1, source_target_pairs={{0,32},{8,40},{64,96},{72,104},{128,160},{136,168},{192,224},{200,... | collective-permute-start | bytes 786440 | tf_op jit(solution)/shard_map/ppermute | solution.py:260
  78.1 6.1 %collective-permute-done.13.other = f32[256,256]{1,0:T(8,128)S(1)} collective-permute-done((f32[256,256]{1,0:T(8,128)S(1)}, f32[256,256]{1,0:T(8,128)S(1)}, u32[]{:S(2)}, u32[]{:S(2)}) %collective-permute-start.13) | collective-permute-done | bytes 262176 | tf_op jit(solution)/shard_map/ppermute | solution.py:260
  85.1 2.1 %collective-permute-start.14 = (f32[256,256]{1,0:T(8,128)S(1)}, f32[256,256]{1,0:T(8,128)S(1)}, u32[]{:S(2)}, u32[]{:S(2)}) collective-permute-start(f32[256,256]{1,0:T(8,128)S(1)} %get-tuple-element.45.part), channel_id=1, source_target_pairs={{0,64},{8,72},{128,192},{136,200},{64,0},{72,8},{192,128},{200,136... | collective-permute-start | bytes 786440 | tf_op jit(solution)/shard_map/ppermute | solution.py:260
  88.3 4.7 %collective-permute-start.23 = (f32[256,384]{1,0:T(8,128)S(1)}, f32[256,384]{1,0:T(8,128)S(1)}, u32[]{:S(2)}, u32[]{:S(2)}) collective-permute-start(f32[256,384]{1,0:T(8,128)S(1)} %get-tuple-element.60.part), channel_id=1, source_target_pairs={{0,128},{8,136},{128,0},{136,8},{1,129},{9,137},{129,1},{137,9},{2... | collective-permute-start | bytes 1179656 | tf_op jit(solution)/shard_map/ppermute | solution.py:260
  93.9 4.1 %collective-permute-start.17 = (f32[256,256]{1,0:T(8,128)S(1)}, f32[256,256]{1,0:T(8,128)S(1)}, u32[]{:S(2)}, u32[]{:S(2)}) collective-permute-start(f32[256,256]{1,0:T(8,128)S(1)} %get-tuple-element.47.part), channel_id=1, source_target_pairs={{0,128},{8,136},{128,0},{136,8},{1,129},{9,137},{129,1},{137,9},{2... | collective-permute-start | bytes 786440 | tf_op jit(solution)/shard_map/ppermute | solution.py:260
  98.1 4.8 %collective-permute-done.23.other = f32[256,384]{1,0:T(8,128)S(1)} collective-permute-done((f32[256,384]{1,0:T(8,128)S(1)}, f32[256,384]{1,0:T(8,128)S(1)}, u32[]{:S(2)}, u32[]{:S(2)}) %collective-permute-start.23) | collective-permute-done | bytes 393248 | tf_op jit(solution)/shard_map/ppermute | solution.py:260
  103.6 5.4 %collective-permute-start.24 = (f32[256,384]{1,0:T(8,128)S(1)}, f32[256,384]{1,0:T(8,128)S(1)}, u32[]{:S(2)}, u32[]{:S(2)}) collective-permute-start(f32[256,384]{1,0:T(8,128)S(1)} %get-tuple-element.64), channel_id=1, source_target_pairs={{0,8},{16,24},{32,40},{48,56},{64,72},{80,88},{96,104},{112,120},{... | collective-permute-start | bytes 1179656 | tf_op jit(solution)/shard_map/ppermute | solution.py:260
  109.7 2.4 %collective-permute-start.18 = (f32[256,256]{1,0:T(8,128)S(1)}, f32[256,256]{1,0:T(8,128)S(1)}, u32[]{:S(2)}, u32[]{:S(2)}) collective-permute-start(f32[256,256]{1,0:T(8,128)S(1)} %get-tuple-element.51), channel_id=1, source_target_pairs={{0,8},{16,24},{32,40},{48,56},{64,72},{80,88},{96,104},{112,120},{... | collective-permute-start | bytes 786440 | tf_op jit(solution)/shard_map/ppermute | solution.py:260
  112.1 3.1 %shard_map.74._ = f32[512,1280]{1,0:T(8,128)} custom-call(f32[512,1280]{1,0:T(8,128)} %slab.3, bf16[2,512,256]{2,1,0:T(8,128)(2,1)S(1)} %get-tuple-element.37.y, bf16[2,256,768]{2,1,0:T(8,128)(2,1)S(1)} %copy-done.2, bf16[2,256,512]{2,1,0:T(8,128)(2,1)S(1)} %get-tuple-element.66.refs_1_), custom_call_target="tpu_custom_call" | custom-call | flops 1000000000 | bytes 3000000 | tf_op jit(solution)/shard_map/pallas_call | solution.py:247
  (64 shorter events, 30.9 us)
Async XLA Ops:
  0.0 32.3 %collective-permute-start.9 = (f32[5,256,256]{2,1,0:T(8,128)}, f32[5,256,256]{2,1,0:T(8,128)S(1)}, u32[]{:S(2)}, u32[]{:S(2)}) collective-permute-start(f32[5,256,256]{2,1,0:T(8,128)} %own_t.5), channel_id=1, source_target_pairs={{0,8},{16,24},{32,40},{48,56},{64,72},{80,88},{96,104},{112,120},{... | collective-permute-start | bytes 3932168 | tf_op jit(solution)/shard_map/ppermute | solution.py:260
  3.2 35.1 %collective-permute-start.8 = (f32[5,256,256]{2,1,0:T(8,128)}, f32[5,256,256]{2,1,0:T(8,128)S(1)}, u32[]{:S(2)}, u32[]{:S(2)}) collective-permute-start(f32[5,256,256]{2,1,0:T(8,128)} %own_y.9), channel_id=1, source_target_pairs={{0,8},{16,24},{32,40},{48,56},{64,72},{80,88},{96,104},{112,120},{... | collective-permute-start | bytes 3932168 | tf_op jit(solution)/shard_map/ppermute | solution.py:260
  4.1 6.6 %collective-permute-start.6 = (f32[32,768]{1,0:T(8,128)S(1)}, f32[32,768]{1,0:T(8,128)S(1)}, u32[]{:S(2)}, u32[]{:S(2)}) collective-permute-start(f32[32,768]{1,0:T(8,128)S(1)} %pad_maximum_fusion.refs_0_), channel_id=1, source_target_pairs={{0,1},{1,2},{2,3},{3,4},{4,5},{5,6},{6,7},{7,0},{8,9},{9,10},{10,1... | collective-permute-start | bytes 294920 | tf_op jit(solution)/shard_map/ppermute | solution.py:219
  4.1 10.3 %collective-permute-start.3 = (f32[32,768]{1,0:T(8,128)S(1)}, f32[32,768]{1,0:T(8,128)S(1)}, u32[]{:S(2)}, u32[]{:S(2)}) collective-permute-start(f32[32,768]{1,0:T(8,128)S(1)} %pad_maximum_fusion.refs_0_), channel_id=1, source_target_pairs={{0,2},{1,3},{2,4},{3,5},{4,6},{5,7},{6,0},{7,1},{8,10},{9,11},{10,... | collective-permute-start | bytes 294920 | tf_op jit(solution)/shard_map/ppermute | solution.py:219
  7.0 7.6 %collective-permute-start.1 = (f32[32,768]{1,0:T(8,128)S(1)}, f32[32,768]{1,0:T(8,128)S(1)}, u32[]{:S(2)}, u32[]{:S(2)}) collective-permute-start(f32[32,768]{1,0:T(8,128)S(1)} %pad_maximum_fusion.refs_0_), channel_id=1, source_target_pairs={{0,6},{1,7},{2,0},{3,1},{4,2},{5,3},{6,4},{7,5},{8,14},{9,15},{10,... | collective-permute-start | bytes 294920 | tf_op jit(solution)/shard_map/ppermute | solution.py:219
  10.7 6.4 %collective-permute-start = (f32[32,768]{1,0:T(8,128)S(1)}, f32[32,768]{1,0:T(8,128)S(1)}, u32[]{:S(2)}, u32[]{:S(2)}) collective-permute-start(f32[32,768]{1,0:T(8,128)S(1)} %pad_maximum_fusion.refs_0_), channel_id=1, source_target_pairs={{0,7},{1,0},{2,1},{3,2},{4,3},{5,4},{6,5},{7,6},{8,15},{9,8},{10,9... | collective-permute-start | bytes 294920 | tf_op jit(solution)/shard_map/ppermute | solution.py:219
  14.4 4.7 %collective-permute-start.5 = (f32[32,768]{1,0:T(8,128)S(1)}, f32[32,768]{1,0:T(8,128)S(1)}, u32[]{:S(2)}, u32[]{:S(2)}) collective-permute-start(f32[32,768]{1,0:T(8,128)S(1)} %collective-permute-done.3.refs_6_), channel_id=1, source_target_pairs={{0,1},{1,2},{2,3},{3,4},{4,5},{5,6},{6,7},{7,0},{8,9},{9,10},{10,1... | collective-permute-start | bytes 294920 | tf_op jit(solution)/shard_map/ppermute | solution.py:219
  14.7 7.5 %collective-permute-start.4 = (f32[32,768]{1,0:T(8,128)S(1)}, f32[32,768]{1,0:T(8,128)S(1)}, u32[]{:S(2)}, u32[]{:S(2)}) collective-permute-start(f32[32,768]{1,0:T(8,128)S(1)} %collective-permute-done.3.refs_6_), channel_id=1, source_target_pairs={{0,2},{1,3},{2,4},{3,5},{4,6},{5,7},{6,0},{7,1},{8,10},{9,11},{10,... | collective-permute-start | bytes 294920 | tf_op jit(solution)/shard_map/ppermute | solution.py:219
  17.0 5.2 %collective-permute-start.2 = (f32[32,768]{1,0:T(8,128)S(1)}, f32[32,768]{1,0:T(8,128)S(1)}, u32[]{:S(2)}, u32[]{:S(2)}) collective-permute-start(f32[32,768]{1,0:T(8,128)S(1)} %collective-permute-done.1.refs_2_), channel_id=1, source_target_pairs={{0,7},{1,0},{2,1},{3,2},{4,3},{5,4},{6,5},{7,6},{8,15},{9,8},{10,9... | collective-permute-start | bytes 294920 | tf_op jit(solution)/shard_map/ppermute | solution.py:219
  28.9 11.9 %collective-permute-start.19 = (f32[256,384]{1,0:T(8,128)}, f32[256,384]{1,0:T(8,128)}, u32[]{:S(2)}, u32[]{:S(2)}) collective-permute-start(f32[256,384]{1,0:T(8,128)} %get-tuple-element.53), channel_id=1, source_target_pairs={{0,8},{16,24},{32,40},{48,56},{64,72},{80,88},{96,104},{112,120},{... | collective-permute-start | bytes 1179656 | tf_op jit(solution)/shard_map/ppermute | solution.py:260
  33.4 10.4 %collective-permute-start.11 = (f32[256,256]{1,0:T(8,128)S(1)}, f32[256,256]{1,0:T(8,128)S(1)}, u32[]{:S(2)}, u32[]{:S(2)}) collective-permute-start(f32[256,256]{1,0:T(8,128)S(1)} %get-tuple-element.68), channel_id=1, source_target_pairs={{0,16},{32,48},{64,80},{96,112},{128,144},{160,176},{192,208},{224... | collective-permute-start | bytes 786440 | tf_op jit(solution)/shard_map/ppermute | solution.py:260
  43.7 10.1 %collective-permute-start.20 = (f32[256,384]{1,0:T(8,128)S(1)}, f32[256,384]{1,0:T(8,128)S(1)}, u32[]{:S(2)}, u32[]{:S(2)}) collective-permute-start(f32[256,384]{1,0:T(8,128)S(1)} %get-tuple-element.54.part), channel_id=1, source_target_pairs={{0,16},{8,24},{32,48},{40,56},{64,80},{72,88},{96,112},{104,120},{... | collective-permute-start | bytes 1179656 | tf_op jit(solution)/shard_map/ppermute | solution.py:260
  46.6 14.8 %collective-permute-start.7 = (f32[256,256]{1,0:T(8,128)S(1)}, f32[256,256]{1,0:T(8,128)S(1)}, u32[]{:S(2)}, u32[]{:S(2)}) collective-permute-start(f32[256,256]{1,0:T(8,128)S(1)} %get-tuple-element.40), channel_id=1, source_target_pairs={{0,8},{16,24},{32,40},{48,56},{64,72},{80,88},{96,104},{112,120},{... | collective-permute-start | bytes 786440 | tf_op jit(solution)/shard_map/ppermute | solution.py:260
  54.8 14.3 %collective-permute-start.21 = (f32[256,384]{1,0:T(8,128)S(1)}, f32[256,384]{1,0:T(8,128)S(1)}, u32[]{:S(2)}, u32[]{:S(2)}) collective-permute-start(f32[256,384]{1,0:T(8,128)S(1)} %get-tuple-element.56.part), channel_id=1, source_target_pairs={{0,32},{8,40},{64,96},{72,104},{128,160},{136,168},{192,224},{200,... | collective-permute-start | bytes 1179656 | tf_op jit(solution)/shard_map/ppermute | solution.py:260
  56.7 10.6 %collective-permute-start.15 = (f32[256,256]{1,0:T(8,128)S(1)}, f32[256,256]{1,0:T(8,128)S(1)}, u32[]{:S(2)}, u32[]{:S(2)}) collective-permute-start(f32[256,256]{1,0:T(8,128)S(1)} %get-tuple-element.67), channel_id=1, source_target_pairs={{0,64},{128,192},{8,136},{1,65},{129,193},{9,137},{2,66},{130,194}... | collective-permute-start | bytes 786440 | tf_op jit(solution)/shard_map/ppermute | solution.py:260
  63.0 10.3 %collective-permute-start.10 = (f32[256,256]{1,0:T(8,128)S(1)}, f32[256,256]{1,0:T(8,128)S(1)}, u32[]{:S(2)}, u32[]{:S(2)}) collective-permute-start(f32[256,256]{1,0:T(8,128)S(1)} %get-tuple-element.41.part), channel_id=1, source_target_pairs={{0,16},{8,24},{32,48},{40,56},{64,80},{72,88},{96,112},{104,120},{... | collective-permute-start | bytes 786440 | tf_op jit(solution)/shard_map/ppermute | solution.py:260
  67.4 10.5 %collective-permute-start.16 = (f32[256,256]{1,0:T(8,128)S(1)}, f32[256,256]{1,0:T(8,128)S(1)}, u32[]{:S(2)}, u32[]{:S(2)}) collective-permute-start(f32[256,256]{1,0:T(8,128)S(1)} %collective-permute-done.15.got), channel_id=1, source_target_pairs={{0,8},{16,24},{32,40},{48,56},{64,72},{80,88},{96,104},{112,120},{... | collective-permute-start | bytes 786440 | tf_op jit(solution)/shard_map/ppermute | solution.py:260
  70.1 17.2 %collective-permute-start.22 = (f32[256,384]{1,0:T(8,128)S(1)}, f32[256,384]{1,0:T(8,128)S(1)}, u32[]{:S(2)}, u32[]{:S(2)}) collective-permute-start(f32[256,384]{1,0:T(8,128)S(1)} %get-tuple-element.58.part), channel_id=1, source_target_pairs={{0,64},{8,72},{128,192},{136,200},{64,0},{72,8},{192,128},{200,136... | collective-permute-start | bytes 1179656 | tf_op jit(solution)/shard_map/ppermute | solution.py:260
  74.2 10.0 %collective-permute-start.13 = (f32[256,256]{1,0:T(8,128)S(1)}, f32[256,256]{1,0:T(8,128)S(1)}, u32[]{:S(2)}, u32[]{:S(2)}) collective-permute-start(f32[256,256]{1,0:T(8,128)S(1)} %get-tuple-element.43.part), channel_id=1, source_target_pairs={{0,32},{8,40},{64,96},{72,104},{128,160},{136,168},{192,224},{200,... | collective-permute-start | bytes 786440 | tf_op jit(solution)/shard_map/ppermute | solution.py:260
  85.1 7.9 %collective-permute-start.14 = (f32[256,256]{1,0:T(8,128)S(1)}, f32[256,256]{1,0:T(8,128)S(1)}, u32[]{:S(2)}, u32[]{:S(2)}) collective-permute-start(f32[256,256]{1,0:T(8,128)S(1)} %get-tuple-element.45.part), channel_id=1, source_target_pairs={{0,64},{8,72},{128,192},{136,200},{64,0},{72,8},{192,128},{200,136... | collective-permute-start | bytes 786440 | tf_op jit(solution)/shard_map/ppermute | solution.py:260
  88.3 14.5 %collective-permute-start.23 = (f32[256,384]{1,0:T(8,128)S(1)}, f32[256,384]{1,0:T(8,128)S(1)}, u32[]{:S(2)}, u32[]{:S(2)}) collective-permute-start(f32[256,384]{1,0:T(8,128)S(1)} %get-tuple-element.60.part), channel_id=1, source_target_pairs={{0,128},{8,136},{128,0},{136,8},{1,129},{9,137},{129,1},{137,9},{2... | collective-permute-start | bytes 1179656 | tf_op jit(solution)/shard_map/ppermute | solution.py:260
  93.9 15.0 %collective-permute-start.17 = (f32[256,256]{1,0:T(8,128)S(1)}, f32[256,256]{1,0:T(8,128)S(1)}, u32[]{:S(2)}, u32[]{:S(2)}) collective-permute-start(f32[256,256]{1,0:T(8,128)S(1)} %get-tuple-element.47.part), channel_id=1, source_target_pairs={{0,128},{8,136},{128,0},{136,8},{1,129},{9,137},{129,1},{137,9},{2... | collective-permute-start | bytes 786440 | tf_op jit(solution)/shard_map/ppermute | solution.py:260
  103.6 11.6 %collective-permute-start.24 = (f32[256,384]{1,0:T(8,128)S(1)}, f32[256,384]{1,0:T(8,128)S(1)}, u32[]{:S(2)}, u32[]{:S(2)}) collective-permute-start(f32[256,384]{1,0:T(8,128)S(1)} %get-tuple-element.64), channel_id=1, source_target_pairs={{0,8},{16,24},{32,40},{48,56},{64,72},{80,88},{96,104},{112,120},{... | collective-permute-start | bytes 1179656 | tf_op jit(solution)/shard_map/ppermute | solution.py:260
  109.7 6.4 %collective-permute-start.18 = (f32[256,256]{1,0:T(8,128)S(1)}, f32[256,256]{1,0:T(8,128)S(1)}, u32[]{:S(2)}, u32[]{:S(2)}) collective-permute-start(f32[256,256]{1,0:T(8,128)S(1)} %get-tuple-element.51), channel_id=1, source_target_pairs={{0,8},{16,24},{32,40},{48,56},{64,72},{80,88},{96,104},{112,120},{... | collective-permute-start | bytes 786440 | tf_op jit(solution)/shard_map/ppermute | solution.py:260
  (8 other events, 16.2 us)
